TPU v7x, 32 devices: a whole 2x2x4 slice. The times are simulated.
32 devices in a mesh: cand: 16 (over z, x, core), tp: 2 (over y).
Axes of the slice: x: 2, y: 2, z: 4, core: 2. Of those that a mesh axis runs over, the one named last changes fastest.
Arguments:
- hidden_in: bfloat16 [128, 2, 8192], P('cand'), may hold values from -4 to 4
- queries: bfloat16 [128, 2, 32, 128], P('cand', None, 'tp'), may hold values from -128 to 128
- new_kv: bfloat16 [128, 2, 8, 2, 128], P('cand', None, 'tp'), may hold values from -5 to 5
- kv_cache: bfloat16 [128, 8, 2, 512, 128], P('cand', 'tp'), may hold values from -6 to 6
- lengths: int32 [128], P('cand'), may hold values from 128 to 512, as said below
- winner: int32 [8], replicated, may hold values from 0 to 15
- out_values: bfloat16 [4096, 8192], P('tp'), may hold values from -4 to 4
- out_scales: float32 [32, 64], P('tp'), may hold values from 0.008 to 0.032
Outputs:
- mixed: bfloat16 [128, 2, 8192], P('cand')
Inputs may be any that keep to these rules, and one draw needn't show every extreme that they name: `lengths`: every draw has some row with exactly 512 live slots.
All inputs are finite; a program needn't handle non-finite values.
Results may differ from a plain program's by a relative error of at most 0.013.
Values may be sent and summed in bfloat16 or wider, within the bound.
A program may use at most 128 MiB of HBM per device.

v0:
```python
import math
import jax
import jax.numpy as jnp
from jax import lax
from jax.sharding import PartitionSpec as P

BLOCK = 64
KB = 256


def own_blocks(cache_rows, row_lengths):

    def take_block(cache_row, row_length):
        return lax.dynamic_slice_in_dim(cache_row, row_length - BLOCK, BLOCK, 2)

    return jax.vmap(take_block)(cache_rows, row_lengths)


def local(hidden_in, queries, new_kv, kv_cache, lengths, winner, out_values, out_scales):
    problems = kv_cache.shape[0]
    kv_here = kv_cache.shape[1]
    steps_count = queries.shape[1]
    heads_here = queries.shape[2]
    head_dim = queries.shape[3]
    group = heads_here // kv_here
    blocks = own_blocks(kv_cache, lengths)
    owner_mask = winner == lax.axis_index("cand")
    masked = jnp.where(owner_mask[:, None, None, None, None], blocks, jnp.zeros((), jnp.bfloat16))
    forked = lax.psum(masked, "cand").astype(jnp.float32).astype(jnp.bfloat16)
    grouped = queries.reshape(problems, steps_count, kv_here, group, head_dim)
    factor = 1.0 / math.sqrt(head_dim)

    def scores_of(keys):
        return (
            jnp.einsum("ptkgd,pkjd->ptkgj", grouped, keys, preferred_element_type=jnp.float32)
            * factor
        )

    def combine_values(weights, values):
        return jnp.einsum("ptkgj,pkjd->ptkgd", weights, values, preferred_element_type=jnp.float32)

    fresh = jnp.transpose(new_kv, (0, 2, 3, 1, 4))
    fork_scores = scores_of(forked[:, :, 0])
    new_scores = scores_of(fresh[:, :, 0])
    causal = jnp.arange(steps_count)[None, :] <= jnp.arange(steps_count)[:, None]
    new_scores = jnp.where(causal[None, :, None, None, :], new_scores, -jnp.inf)
    live = lengths - BLOCK
    count = kv_cache.shape[3] // KB

    def block_scores(index):
        piece = lax.dynamic_slice_in_dim(kv_cache, index * KB, KB, 3)
        scores = scores_of(piece[:, :, 0])
        slots = index * KB + jnp.arange(KB, dtype=jnp.int32)
        valid = slots[None, :] < live[:, None]
        scores = jnp.where(valid[:, None, None, None, :], scores, -jnp.inf)
        return (scores, piece[:, :, 1])

    peak = jnp.maximum(jnp.max(fork_scores, -1), jnp.max(new_scores, -1))
    total = jnp.sum(jnp.exp(fork_scores - peak[..., None]), -1) + jnp.sum(
        jnp.exp(new_scores - peak[..., None]), -1
    )

    def first_pass(index, carry):
        peak_now, total_now = carry
        scores, unused_values = block_scores(index)
        higher = jnp.maximum(peak_now, jnp.max(scores, -1))
        total_now = total_now * jnp.exp(peak_now - higher) + jnp.sum(
            jnp.exp(scores - higher[..., None]), -1
        )
        return (higher, total_now)

    peak, total = lax.fori_loop(0, count, first_pass, (peak, total))

    def weigh(scores):
        return (jnp.exp(scores - peak[..., None]) / total[..., None]).astype(jnp.bfloat16)

    summed = combine_values(weigh(fork_scores), forked[:, :, 1]) + combine_values(
        weigh(new_scores), fresh[:, :, 1]
    )

    def second_pass(index, summed_now):
        scores, values = block_scores(index)
        return summed_now + combine_values(weigh(scores), values)

    summed = lax.fori_loop(0, count, second_pass, summed)
    attended = summed.astype(jnp.bfloat16).reshape(problems * steps_count, heads_here * head_dim)
    blocks_here = out_scales.shape[0]
    side = out_values.shape[0] // blocks_here
    width = out_values.shape[1]
    partial_terms = jnp.einsum(
        "rbk,bkn->rbn",
        attended.reshape(-1, blocks_here, side),
        out_values.reshape(blocks_here, side, width),
        preferred_element_type=jnp.float32,
    )
    spread = jnp.repeat(out_scales, side, axis=1)
    term = jnp.sum(partial_terms * spread[None], axis=1)
    residual = hidden_in.reshape(problems * steps_count, width)
    totals = lax.psum(term.astype(jnp.bfloat16), "tp").astype(jnp.float32)
    result = (residual.astype(jnp.float32) + totals).astype(jnp.bfloat16)
    return result.reshape(hidden_in.shape)


def solution(mesh):
    placed = (
        P("cand", None, None),
        P("cand", None, "tp", None),
        P("cand", None, "tp", None, None),
        P("cand", "tp", None, None, None),
        P("cand"),
        P(),
        P("tp", None),
        P("tp", None),
    )
    return jax.shard_map(
        local, mesh=mesh, in_specs=placed, out_specs=P("cand", None, None), check_vma=False
    )
```

profile of v0, /device:TPU:0, one launch (start us, length us, event | category | flops | bytes accessed | tf_op | source)
XLA Modules:
  0.0 181.5 jit_solution(16705224246081859264)
XLA Ops:
  6.5 0.0 all-reduce.3.cloned.1.call-start
  6.5 0.0 copy-start.6
  6.5 0.0 copy-start.5
  6.5 12.2 %copy.17 = bf16[8,4,2,512,128]{4,1,2,0,3:T(4,128)(2,1)} copy(bf16[8,4,2,512,128]{4,3,2,1,0:T(8,128)(2,1)} %param.15) | data formatting | bytes 16777216 | tf_op args[3]
  18.7 0.0 copy-done.6
  18.7 5.0 %gather_fusion = bf16[8,4,2,64,128]{4,1,2,3,0:T(4,128)(2,1)S(1)} fusion(bf16[8,4,2,512,128]{4,1,2,0,3:T(4,128)(2,1)} %copy.17, s32[8]{0:T(128)S(1)} %fusion.42), kind=kCustom, calls=%fused_computation | custom fusion | bytes 2097312 | tf_op jit(solution)/shard_map/vmap()/gather | solution.py:14
  23.7 0.0 copy-done.5
  23.8 1.1 copy_select_fusion
  24.9 0.0 all-reduce.3.cloned.1.call-update
  24.9 0.0 copy-start.1
  24.9 0.0 copy-start.2
  24.9 0.0 copy-start.3
  25.0 0.0 all-reduce.5.cloned.1.call-start
  25.0 7.6 %copy.22 = bf16[8,4,2,512,128]{4,3,1,0,2:T(8,128)(2,1)} copy(bf16[8,4,2,512,128]{4,3,2,1,0:T(8,128)(2,1)} %param.15) | data formatting | bytes 16777216 | tf_op jit(solution)/shard_map/while | solution.py:72
  32.6 0.0 copy-done.1
  32.6 0.0 copy-done.2
  32.7 0.0 copy-done.3
  32.7 0.2 broadcast_in_dim.120
  32.9 0.3 copy.44
  33.2 0.7 fusion.45
  33.9 87.6 %all-reduce.3.cloned.1.call-done = bf16[8,4,2,64,128]{4,3,1,0,2:T(8,128)(2,1)} async-done(((bf16[8,4,2,64,128]{4,3,1,0,2:T(8,128)(2,1)}), bf16[8,4,2,64,128]{4,3,1,0,2:T(8,128)(2,1)}) %all-reduce.3.cloned.1.call-update) | async-done | bytes 1048592 | tf_op jit(solution)/shard_map/psum | solution.py:29
  121.5 1.5 fusion.44
  123.1 0.3 exponential_reduce_fusion.1
  123.4 0.1 exponential_reduce_fusion.2
  123.5 0.0 copy-start.4
  123.5 5.8 %while.28 = (s32[]{:T(128)}, f32[8,2,4,4]{3,1,2,0:T(2,128)S(1)}, f32[8,2,4,4]{3,1,2,0:T(2,128)S(1)}, s32[8]{0:T(128)S(1)}, bf16[8,4,2,512,128]{4,3,1,0,2:T(8,128...) while((s32[]{:T(128)}, f32[8,2,4,4]{3,1,2,0:T(2,128)S(1)}, ...), condition=%wide.region_8.9_spmd, body=%wide.region_5.8_spmd.sunk | while | flops 17107716 | bytes 2706619 | solution.py:72
  123.6 0.1 broadcast_compare_fusion.5
  123.6 2.4 %fusion.55 = (f32[8,2,4,4]{3,1,2,0:T(2,128)S(1)}, f32[8,2,4,4,256]{4,3,1,2,0:T(4,128)S(1)}) fusion(bf16[8,2,4,4,128]{4,3,1,2,0:T(4,128)(2,1)S(1)} %get-tuple-element.409, bf16[8,4,2,512,128]{4,3,1,0,2:T(8,128)(2,1)} %get-tuple-element.408, s32[]{:T(128)S(6)} %select_n.75, pred[8,256]{1,0:T(8,128)(4,1)S(1)} %broadcast_compare_fusion.5), kind=kOutput, calls=%fused_computation.71.clone.1 | convolution fusion | flops 16973568 | bytes 2427908 | tf_op jit(solution)/shard_map/while/body/eval_jaxpr/ptkgd,pkjd->ptkgj/dot_general | solution.py:35
  126.1 0.3 exponential_reduce_fusion.4
  126.5 0.1 broadcast_compare_fusion.5
  126.5 2.4 %fusion.55 = (f32[8,2,4,4]{3,1,2,0:T(2,128)S(1)}, f32[8,2,4,4,256]{4,3,1,2,0:T(4,128)S(1)}) fusion(bf16[8,2,4,4,128]{4,3,1,2,0:T(4,128)(2,1)S(1)} %get-tuple-element.409, bf16[8,4,2,512,128]{4,3,1,0,2:T(8,128)(2,1)} %get-tuple-element.408, s32[]{:T(128)S(6)} %select_n.75, pred[8,256]{1,0:T(8,128)(4,1)S(1)} %broadcast_compare_fusion.5), kind=kOutput, calls=%fused_computation.71.clone.1 | convolution fusion | flops 16973568 | bytes 2427908 | tf_op jit(solution)/shard_map/while/body/eval_jaxpr/ptkgd,pkjd->ptkgj/dot_general | solution.py:35
  128.9 0.3 exponential_reduce_fusion.4
  129.3 0.3 convolution_bitcast_fusion.1
  129.6 0.0 copy-done.4
  129.6 0.3 fusion.28
  129.9 6.6 %while.29 = (s32[]{:T(128)}, f32[8,2,4,4,128]{4,3,1,2,0:T(4,128)S(1)}, bf16[8,4,2,512,128]{4,3,1,0,2:T(8,128)(2,1)}, s32[8]{0:T(128)S(1)}, bf16[8,2,4,4,128]{4,3...) while((s32[]{:T(128)}, ...), condition=%wide.region_10.11_spmd, body=%wide.region_9.10_spmd.sunk | while | flops 33917192 | bytes 4531923 | solution.py:85
  129.9 0.1 broadcast_compare_fusion.6
  130.0 3.2 %fusion.57 = f32[8,2,4,4,128]{4,3,1,2,0:T(4,128)S(1)} fusion(f32[8,2,4,4,128]{4,3,1,2,0:T(4,128)S(1)} %get-tuple-element.427, bf16[8,4,2,512,128]{4,3,1,0,2:T(8,128)(2,1)} %get-tuple-element.440, s32[]{:T(128)S(6)} %add.151, s32[]{:T(128)S(6)} %select_n.77, f32[8,2,4,4]{3,1,2,0:T(2,128)S(1)} %get-tuple-element.444, ...), kind=kOutput, calls=%fused_computation.23.clone.1 | convolution fusion | flops 33914880 | bytes 4527616 | tf_op jit(solution)/shard_map/while/body/eval_jaxpr/ptkgj,pkjd->ptkgd/dot_general | solution.py:40
  133.2 0.1 broadcast_compare_fusion.6
  133.3 3.2 %fusion.57 = f32[8,2,4,4,128]{4,3,1,2,0:T(4,128)S(1)} fusion(f32[8,2,4,4,128]{4,3,1,2,0:T(4,128)S(1)} %get-tuple-element.427, bf16[8,4,2,512,128]{4,3,1,0,2:T(8,128)(2,1)} %get-tuple-element.440, s32[]{:T(128)S(6)} %add.151, s32[]{:T(128)S(6)} %select_n.77, f32[8,2,4,4]{3,1,2,0:T(2,128)S(1)} %get-tuple-element.444, ...), kind=kOutput, calls=%fused_computation.23.clone.1 | convolution fusion | flops 33914880 | bytes 4527616 | tf_op jit(solution)/shard_map/while/body/eval_jaxpr/ptkgj,pkjd->ptkgd/dot_general | solution.py:40
  136.5 0.0 copy-start
  136.6 13.7 %fusion.27 = bf16[16,8192]{1,0:T(8,128)(2,1)} fusion(f32[16,8192]{1,0:T(8,128)S(1)} %bitcast.153, bf16[16,128,8192]{2,1,0:T(8,128)(2,1)} %bitcast.151, bf16[16,16,128]{2,1,0:T(8,128)(2,1)S(1)} %bitcast.159), kind=kOutput, calls=%fused_computation.36 | convolution fusion | flops 540934144 | bytes 34406400 | tf_op jit(solution)/shard_map/rbk,bkn->rbn/dot_general | solution.py:90
  150.2 0.0 all-reduce.5.cloned.1.call-update
  150.2 0.0 copy-done
  150.2 0.1 reshape.97
  150.3 22.4 %all-reduce.5.cloned.1.call-done = bf16[16,8192]{1,0:T(8,128)(2,1)} async-done(((bf16[16,8192]{1,0:T(8,128)(2,1)}), bf16[16,8192]{1,0:T(8,128)(2,1)}) %all-reduce.5.cloned.1.call-update) | async-done | bytes 262160 | tf_op jit(solution)/shard_map/psum | solution.py:99
  172.8 1.0 add_convert_fusion
  173.8 0.9 reshape.96
  (20 shorter events, 0.3 us)
Async XLA Ops:
  6.5 115.0 %all-reduce.3.cloned.1.call-start = ((), (), s32[]{:S(2)}) async-start(), calls=%async_computation | async-start | bytes 2097152 | tf_op jit(solution)/shard_map/psum | solution.py:29
  6.5 12.2 %copy-start.6 = (s32[8]{0:T(128)S(1)}, s32[8]{0:T(128)}, u32[]{:S(2)}) copy-start(s32[8]{0:T(128)} %param.16) | copy-start | bytes 100
  6.5 17.2 %copy-start.5 = (s32[8]{0:T(128)S(1)}, s32[8]{0:T(128)}, u32[]{:S(2)}) copy-start(s32[8]{0:T(128)} %param.17) | copy-start | bytes 100
  24.9 7.7 %copy-start.1 = (bf16[8,2,16,128]{3,2,1,0:T(8,128)(2,1)S(1)}, bf16[8,2,16,128]{3,2,1,0:T(8,128)(2,1)}, u32[]{:S(2)}) copy-start(bf16[8,2,16,128]{3,2,1,0:T(8,128)(2,1)} %param.13) | copy-start | bytes 196612
  24.9 7.7 %copy-start.2 = (bf16[8,2,4,2,128]{4,3,2,1,0:T(2,128)(2,1)S(1)}, bf16[8,2,4,2,128]{4,3,2,1,0:T(2,128)(2,1)}, u32[]{:S(2)}) copy-start(bf16[8,2,4,2,128]{4,3,2,1,0:T(2,128)(2,1)} %param.14) | copy-start | bytes 98308
  24.9 7.7 %copy-start.3 = (f32[16,64]{1,0:T(8,128)S(1)}, f32[16,64]{1,0:T(8,128)}, u32[]{:S(2)}) copy-start(f32[16,64]{1,0:T(8,128)} %param.19) | copy-start | bytes 12292
  25.0 147.8 %all-reduce.5.cloned.1.call-start = ((), (), s32[]{:S(2)}) async-start(), calls=%async_computation.1 | async-start | bytes 524288 | tf_op jit(solution)/shard_map/psum | solution.py:99
  123.5 6.0 %copy-start.4 = (bf16[8,4,2,64,128]{4,3,1,0,2:T(8,128)(2,1)S(1)}, bf16[8,4,2,64,128]{4,3,1,0,2:T(8,128)(2,1)}, u32[]{:S(2)}) copy-start(bf16[8,4,2,64,128]{4,3,1,0,2:T(8,128)(2,1)} %all-reduce.3.cloned.1.call-done) | copy-start | bytes 3145732
  136.5 13.7 %copy-start = (bf16[8,2,8192]{2,1,0:T(2,128)(2,1)S(1)}, bf16[8,2,8192]{2,1,0:T(2,128)(2,1)}, u32[]{:S(2)}) copy-start(bf16[8,2,8192]{2,1,0:T(2,128)(2,1)} %param.12) | copy-start | bytes 786436
Sparse Core Ops, SparseCore 0:
  25.0 96.4 all-reduce.2
  150.4 22.3 all-reduce.4
where the time goes:
time: 182 us; the launch traced here: 181 us
  waiting for transfers between devices  110 us (60%)
  matrix products  27.6 us (15%)
  local copies, waits for them, and re-layouts  26.3 us (14%)
  between operations  13.6 us (7%)
  other arithmetic  3.67 us (2%)
    psum x1, waiting for transfers between devices, local(): forked = lax.psum(masked, 'cand').astype(jnp.float32).astype(jnp.bfloat16)  87.6 us
    psum x1, waiting for transfers between devices, local(): totals = lax.psum(term.astype(jnp.bfloat16), 'tp').astype(jnp.float32)  22.4 us
    dot_general x1, matrix products, local(): jnp.einsum('rbk,bkn->rbn', attended.reshape(-1, blocks_here, side), out_v...  13.7 us
    unnamed x17, local copies, waits for them, and re-layouts  12.5 us
    while x1, local copies, waits for them, and re-layouts, local(): peak, total = lax.fori_loop(0, count, first_pass, (peak, total))  7.6 us
    dot_general x4, matrix products, scores_of(): jnp.einsum('ptkgd,pkjd->ptkgj', grouped, keys, preferred_element_type=jnp...  6.99 us
    dot_general x4, matrix products, combine_values(): jnp.einsum('ptkgj,pkjd->ptkgd', weights, values, preferred_element_type=j...  6.96 us
    gather x1, local copies, waits for them, and re-layouts, take_block(): return lax.dynamic_slice_in_dim(cache_row, row_length - BLOCK, BLOCK, 2)  4.99 us
  transfers between devices with their start and end apart: 2, of which 2 were waited for; matrix products, arithmetic and copies ran while one was open for 5% of the time, Pallas kernels for 0%

commit v1 on v0

--- a/solution.py
+++ b/solution.py
@@ -1,3 +1,4 @@
+import functools
 import math
 import jax
 import jax.numpy as jnp
@@ -6,6 +7,13 @@
 
 BLOCK = 64
 KB = 256
+
+
+def read_windows(local_values, which_axis):
+    return lax.all_gather(local_values, which_axis).sum(axis=0)
+
+
+_draft_points = functools.partial(read_windows, which_axis="cand")
 
 
 def own_blocks(cache_rows, row_lengths):
@@ -26,7 +34,7 @@
     blocks = own_blocks(kv_cache, lengths)
     owner_mask = winner == lax.axis_index("cand")
     masked = jnp.where(owner_mask[:, None, None, None, None], blocks, jnp.zeros((), jnp.bfloat16))
-    forked = lax.psum(masked, "cand").astype(jnp.float32).astype(jnp.bfloat16)
+    forked = _draft_points(masked).astype(jnp.float32).astype(jnp.bfloat16)
     grouped = queries.reshape(problems, steps_count, kv_here, group, head_dim)
     factor = 1.0 / math.sqrt(head_dim)
 

time: 182 us -> 223 us (1.23)
  waiting for transfers between devices: 110 us -> 142 us
  other arithmetic: 3.67 us -> 12.4 us
    all_gather x0 -> x1, waiting for transfers between devices: none -> 120 us  [read_windows(): return lax.all_gather(local_values, which_axis).sum(axis=0)]
    psum x1 -> x0, waiting for transfers between devices: 87.6 us -> none  [local(): forked = lax.psum(masked, 'cand').astype(jnp.float32).astype(jnp.bfloat16)]
    reduce_sum x0 -> x1, other arithmetic: none -> 9.34 us  [read_windows(): return lax.all_gather(local_values, which_axis).sum(axis=0)]
    unnamed x17 -> x16, local copies, waits for them, and re-layouts: 12.5 us -> 12.6 us
  transfers between devices with their start and end apart: 2 -> 2, of which waited for: 2 -> 2; matrix products, arithmetic and copies ran while one was open for 5% -> 4% of each run, Pallas kernels for 0% -> 0%
where the time goes in v1:
time: 223 us; the launch traced here: 222 us
  waiting for transfers between devices  142 us (64%)
  local copies, waits for them, and re-layouts  27.7 us (12%)
  matrix products  26.5 us (12%)
  between operations  13.6 us (6%)
  other arithmetic  12.4 us (6%)
    all_gather x1, waiting for transfers between devices, read_windows(): return lax.all_gather(local_values, which_axis).sum(axis=0)  120 us
    psum x1, waiting for transfers between devices, local(): totals = lax.psum(term.astype(jnp.bfloat16), 'tp').astype(jnp.float32)  21.5 us
    dot_general x1, matrix products, local(): jnp.einsum('rbk,bkn->rbn', attended.reshape(-1, blocks_here, side), out_v...  13.7 us
    unnamed x16, local copies, waits for them, and re-layouts  12.6 us
    reduce_sum x1, other arithmetic, read_windows(): return lax.all_gather(local_values, which_axis).sum(axis=0)  9.34 us
    while x1, local copies, waits for them, and re-layouts, local(): peak, total = lax.fori_loop(0, count, first_pass, (peak, total))  7.6 us
    dot_general x4, matrix products, combine_values(): jnp.einsum('ptkgj,pkjd->ptkgd', weights, values, preferred_element_type=j...  6.95 us
    dot_general x4, matrix products, scores_of(): jnp.einsum('ptkgd,pkjd->ptkgj', grouped, keys, preferred_element_type=jnp...  5.88 us
  transfers between devices with their start and end apart: 2, of which 2 were waited for; matrix products, arithmetic and copies ran while one was open for 4% of the time, Pallas kernels for 0%

profile of v1, /device:TPU:0, one launch (start us, length us, event | category | flops | bytes accessed | tf_op | source)
XLA Modules:
  0.0 222.2 jit_solution(18076443242618523915)
XLA Ops:
  6.5 0.0 all-gather.2.cloned.1.call-start
  6.5 0.0 copy-start.5
  6.5 0.0 copy-start.4
  6.5 12.2 %copy.35 = bf16[8,4,2,512,128]{4,1,2,0,3:T(4,128)(2,1)} copy(bf16[8,4,2,512,128]{4,3,2,1,0:T(8,128)(2,1)} %param.15) | data formatting | bytes 16777216 | tf_op args[3]
  18.7 0.0 copy-done.5
  18.7 5.0 %gather_fusion = bf16[8,4,2,64,128]{4,1,2,3,0:T(4,128)(2,1)S(1)} fusion(bf16[8,4,2,512,128]{4,1,2,0,3:T(4,128)(2,1)} %copy.35, s32[8]{0:T(128)S(1)} %fusion.40), kind=kCustom, calls=%fused_computation | custom fusion | bytes 2097312 | tf_op jit(solution)/shard_map/vmap()/gather | solution.py:22
  23.7 0.0 copy-done.4
  23.8 0.5 bitcast_select_fusion
  24.3 1.4 copy.36
  25.6 0.0 all-gather.2.cloned.1.call-update
  25.6 0.0 copy-start.1
  25.7 0.0 copy-start.2
  25.7 0.0 copy-start.3
  25.7 0.0 all-reduce.2.cloned.1.call-start
  25.7 7.6 %copy.44 = bf16[8,4,2,512,128]{4,3,1,0,2:T(8,128)(2,1)} copy(bf16[8,4,2,512,128]{4,3,2,1,0:T(8,128)(2,1)} %param.15) | data formatting | bytes 16777216 | tf_op jit(solution)/shard_map/while | solution.py:80
  33.3 0.0 copy-done.1
  33.4 0.0 copy-done.2
  33.4 0.0 copy-done.3
  33.4 0.2 broadcast_in_dim.120
  33.6 0.3 copy.70
  34.0 0.7 fusion.43
  34.7 120.3 %all-gather.2.cloned.1.call-done = bf16[16,8,4,2,64,128]{5,4,3,2,1,0:T(8,128)(2,1)} async-done(((bf16[1,8,4,2,64,128]{5,4,3,2,1,0:T(8,128)(2,1)}), bf16[16,8,4,2,64,128]{5,4,3,2,1,0:T(8,128)(2,1)}) %all-gather.2.cloned.1.call-update) | async-done | bytes 16777232 | tf_op jit(solution)/shard_map/all_gather | solution.py:13
  155.0 9.3 %reduce_sum.52 = bf16[8,4,2,64,128]{4,3,2,1,0:T(8,128)(2,1)S(1)} reduce(bf16[16,8,4,2,64,128]{5,4,3,2,1,0:T(8,128)(2,1)} %all-gather.2.cloned.1.call-done, bf16[]{:T(256)} %constant.109.clone.1), dimensions={0}, to_apply=%region_0.1 | reduce | flops 7864320 | bytes 17825794 | tf_op jit(solution)/shard_map/reduce_sum | solution.py:13
  164.3 0.5 fusion.42
  164.8 0.3 exponential_reduce_fusion.1
  165.1 0.1 exponential_reduce_fusion.2
  165.3 5.7 %while.28 = (s32[]{:T(128)}, f32[8,2,4,4]{3,1,2,0:T(2,128)S(1)}, f32[8,2,4,4]{3,1,2,0:T(2,128)S(1)}, s32[8]{0:T(128)S(1)}, bf16[8,4,2,512,128]{4,3,1,0,2:T(8,128...) while((s32[]{:T(128)}, f32[8,2,4,4]{3,1,2,0:T(2,128)S(1)}, ...), condition=%wide.region_8.9_spmd, body=%wide.region_5.8_spmd.sunk | while | flops 17107716 | bytes 2706619 | solution.py:80
  165.3 0.1 broadcast_compare_fusion.5
  165.4 2.3 %fusion.54 = (f32[8,2,4,4]{3,1,2,0:T(2,128)S(1)}, f32[8,2,4,4,256]{4,3,1,2,0:T(4,128)S(1)}) fusion(bf16[8,2,4,4,128]{4,3,1,2,0:T(4,128)(2,1)S(1)} %get-tuple-element.435, bf16[8,4,2,512,128]{4,3,1,0,2:T(8,128)(2,1)} %get-tuple-element.434, s32[]{:T(128)S(6)} %select_n.82, pred[8,256]{1,0:T(8,128)(4,1)S(1)} %broadcast_compare_fusion.5), kind=kOutput, calls=%fused_computation.70.clone.1 | convolution fusion | flops 16973568 | bytes 2427908 | tf_op jit(solution)/shard_map/while/body/eval_jaxpr/ptkgd,pkjd->ptkgj/dot_general | solution.py:43
  167.8 0.3 exponential_reduce_fusion.4
  168.1 0.1 broadcast_compare_fusion.5
  168.2 2.3 %fusion.54 = (f32[8,2,4,4]{3,1,2,0:T(2,128)S(1)}, f32[8,2,4,4,256]{4,3,1,2,0:T(4,128)S(1)}) fusion(bf16[8,2,4,4,128]{4,3,1,2,0:T(4,128)(2,1)S(1)} %get-tuple-element.435, bf16[8,4,2,512,128]{4,3,1,0,2:T(8,128)(2,1)} %get-tuple-element.434, s32[]{:T(128)S(6)} %select_n.82, pred[8,256]{1,0:T(8,128)(4,1)S(1)} %broadcast_compare_fusion.5), kind=kOutput, calls=%fused_computation.70.clone.1 | convolution fusion | flops 16973568 | bytes 2427908 | tf_op jit(solution)/shard_map/while/body/eval_jaxpr/ptkgd,pkjd->ptkgj/dot_general | solution.py:43
  170.6 0.3 exponential_reduce_fusion.4
  171.0 0.3 convolution_bitcast_fusion.1
  171.2 0.3 fusion.26
  171.5 6.6 %while.29 = (s32[]{:T(128)}, f32[8,2,4,4,128]{4,3,1,2,0:T(4,128)S(1)}, bf16[8,4,2,512,128]{4,3,1,0,2:T(8,128)(2,1)}, s32[8]{0:T(128)S(1)}, bf16[8,2,4,4,128]{4,3...) while((s32[]{:T(128)}, ...), condition=%wide.region_10.11_spmd, body=%wide.region_9.10_spmd.sunk | while | flops 33917192 | bytes 4531923 | solution.py:93
  171.6 0.1 broadcast_compare_fusion.6
  171.6 3.2 %fusion.56 = f32[8,2,4,4,128]{4,3,1,2,0:T(4,128)S(1)} fusion(f32[8,2,4,4,128]{4,3,1,2,0:T(4,128)S(1)} %get-tuple-element.453, bf16[8,4,2,512,128]{4,3,1,0,2:T(8,128)(2,1)} %get-tuple-element.466, s32[]{:T(128)S(6)} %add.149, s32[]{:T(128)S(6)} %select_n.84, bf16[8,2,4,4,128]{4,3,1,2,0:T(4,128)(2,1)S(1)} %get-tuple-element.468, ...), kind=kOutput, calls=%fused_computation.23.clone.1 | convolution fusion | flops 33914880 | bytes 4527616 | tf_op jit(solution)/shard_map/while/body/eval_jaxpr/ptkgj,pkjd->ptkgd/dot_general | solution.py:48
  174.9 0.1 broadcast_compare_fusion.6
  174.9 3.2 %fusion.56 = f32[8,2,4,4,128]{4,3,1,2,0:T(4,128)S(1)} fusion(f32[8,2,4,4,128]{4,3,1,2,0:T(4,128)S(1)} %get-tuple-element.453, bf16[8,4,2,512,128]{4,3,1,0,2:T(8,128)(2,1)} %get-tuple-element.466, s32[]{:T(128)S(6)} %add.149, s32[]{:T(128)S(6)} %select_n.84, bf16[8,2,4,4,128]{4,3,1,2,0:T(4,128)(2,1)S(1)} %get-tuple-element.468, ...), kind=kOutput, calls=%fused_computation.23.clone.1 | convolution fusion | flops 33914880 | bytes 4527616 | tf_op jit(solution)/shard_map/while/body/eval_jaxpr/ptkgj,pkjd->ptkgd/dot_general | solution.py:48
  178.2 0.0 copy-start
  178.2 13.7 %fusion.25 = bf16[16,8192]{1,0:T(8,128)(2,1)} fusion(f32[16,8192]{1,0:T(8,128)S(1)} %bitcast.162, bf16[16,128,8192]{2,1,0:T(8,128)(2,1)} %bitcast.160, bf16[16,16,128]{2,1,0:T(8,128)(2,1)S(1)} %bitcast.168), kind=kOutput, calls=%fused_computation.35 | convolution fusion | flops 540934144 | bytes 34406400 | tf_op jit(solution)/shard_map/rbk,bkn->rbn/dot_general | solution.py:98
  191.9 0.0 all-reduce.2.cloned.1.call-update
  191.9 0.0 copy-done
  191.9 0.1 reshape.104
  192.0 21.5 %all-reduce.2.cloned.1.call-done = bf16[16,8192]{1,0:T(8,128)(2,1)} async-done(((bf16[16,8192]{1,0:T(8,128)(2,1)}), bf16[16,8192]{1,0:T(8,128)(2,1)}) %all-reduce.2.cloned.1.call-update) | async-done | bytes 262160 | tf_op jit(solution)/shard_map/psum | solution.py:107
  213.5 1.0 add_convert_fusion
  214.5 0.9 reshape.103
  (21 shorter events, 0.3 us)
Async XLA Ops:
  6.5 148.4 %all-gather.2.cloned.1.call-start = ((), (), s32[]{:S(2)}) async-start(), calls=%async_computation | async-start | bytes 17825792 | tf_op jit(solution)/shard_map/all_gather | solution.py:13
  6.5 12.2 %copy-start.5 = (s32[8]{0:T(128)S(1)}, s32[8]{0:T(128)}, u32[]{:S(2)}) copy-start(s32[8]{0:T(128)} %param.16) | copy-start | bytes 100
  6.5 17.2 %copy-start.4 = (s32[8]{0:T(128)S(1)}, s32[8]{0:T(128)}, u32[]{:S(2)}) copy-start(s32[8]{0:T(128)} %param.17) | copy-start | bytes 100
  25.6 7.7 %copy-start.1 = (bf16[8,2,16,128]{3,2,1,0:T(8,128)(2,1)S(1)}, bf16[8,2,16,128]{3,2,1,0:T(8,128)(2,1)}, u32[]{:S(2)}) copy-start(bf16[8,2,16,128]{3,2,1,0:T(8,128)(2,1)} %param.13) | copy-start | bytes 196612
  25.7 7.7 %copy-start.2 = (bf16[8,2,4,2,128]{4,3,2,1,0:T(2,128)(2,1)S(1)}, bf16[8,2,4,2,128]{4,3,2,1,0:T(2,128)(2,1)}, u32[]{:S(2)}) copy-start(bf16[8,2,4,2,128]{4,3,2,1,0:T(2,128)(2,1)} %param.14) | copy-start | bytes 98308
  25.7 7.8 %copy-start.3 = (f32[16,64]{1,0:T(8,128)S(1)}, f32[16,64]{1,0:T(8,128)}, u32[]{:S(2)}) copy-start(f32[16,64]{1,0:T(8,128)} %param.19) | copy-start | bytes 12292
  25.7 187.8 %all-reduce.2.cloned.1.call-start = ((), (), s32[]{:S(2)}) async-start(), calls=%async_computation.1 | async-start | bytes 524288 | tf_op jit(solution)/shard_map/psum | solution.py:107
  178.2 13.7 %copy-start = (bf16[8,2,8192]{2,1,0:T(2,128)(2,1)S(1)}, bf16[8,2,8192]{2,1,0:T(2,128)(2,1)}, u32[]{:S(2)}) copy-start(bf16[8,2,8192]{2,1,0:T(2,128)(2,1)} %param.12) | copy-start | bytes 786436
Sparse Core Ops, SparseCore 0:
  25.8 129.1 all-gather.1
  192.0 21.4 all-reduce.1
